TPU v7x, 256 devices: a whole 4x4x8 slice. The times are simulated.
256 devices in a mesh: dp: 4 (over y), tensor: 16 (over z, core), owner: 4 (over x).
Axes of the slice: x: 4, y: 4, z: 8, core: 2. Of those that a mesh axis runs over, the one named last changes fastest.
Arguments:
- queries: bfloat16 [512, 8192], P(('dp', 'tensor'), 'owner'), may hold values from -360 to 360
- cached_key_rows: bfloat16 [512, 512, 8, 128], P(('dp', 'tensor'), None, 'owner'), may hold values from -6 to 6
- cached_value_rows: bfloat16 [512, 512, 8, 128], P(('dp', 'tensor'), None, 'owner'), may hold values from -6 to 6
- newest_key: bfloat16 [512, 8, 128], P(('dp', 'tensor'), 'owner'), may hold values from -6 to 6
- newest_value: bfloat16 [512, 8, 128], P(('dp', 'tensor'), 'owner'), may hold values from -6 to 6
- output_weight: bfloat16 [8, 1024, 8192], P('owner', 'tensor'), may hold values from -0.75 to 0.75
- adapter_down_weight: bfloat16 [128, 8, 1024, 64], P('owner', None, 'tensor'), may hold values from -0.5 to 0.5
- adapter_up_weight: bfloat16 [128, 64, 8192], P('owner', None, 'tensor'), may hold values from -0.75 to 0.75
- adapter_store_row: int32 [128], replicated, may hold values from 0 to 127, each once
- adapters_by_group: int32 [4, 16], P('dp'), may hold values from 0 to 127, as said below
- adapter_per_row: int32 [512], P('dp'), may hold values from 0 to 127, as said below
Outputs:
- output: bfloat16 [512, 8192], P('dp', ('tensor', 'owner'))
Inputs may be any that keep to these rules, and one draw needn't show every extreme that they name: `adapter_per_row`: the rows g * 128 to (g + 1) * 128 - 1 form dp group g; each row's adapter is one of its group's listed adapters, and each listed one is used by some row of the group. `adapters_by_group`: the 16 adapters of a group are distinct.
All inputs are finite; a program needn't handle non-finite values.
Results may differ from a plain program's by a relative error of at most 0.015.
Values may be sent and summed in bfloat16 or wider, within the bound.
No kernel may reach another device: no remote copies, remote signals or barrier semaphores. Data moves between devices by JAX's collectives and lax.ppermute only.
A program may use at most 128 MiB of HBM per device.

v0:
```python
import jax
import jax.numpy as jnp
from jax import lax
from jax.sharding import PartitionSpec as P

ADAPTER_SCALE = 2.0


def shards(
    queries,
    cached_key_rows,
    cached_value_rows,
    newest_key,
    newest_value,
    output_weight,
    adapter_down_weight,
    adapter_up_weight,
    adapter_store_row,
    adapters_by_group,
    adapter_per_row,
):
    owner_index = lax.axis_index("owner")
    row_count = queries.shape[0]
    local_heads = newest_key.shape[1]
    head_width = newest_key.shape[2]
    group_width = queries.shape[1] // local_heads
    query_heads = queries.reshape(row_count, local_heads, group_width // head_width, head_width)
    inverse_root = head_width ** (-0.5)
    scores = (
        jnp.einsum(
            "rkgh,rckh->rkgc", query_heads, cached_key_rows, preferred_element_type=jnp.float32
        )
        * inverse_root
    )
    fresh_score = (
        jnp.einsum("rkgh,rkh->rkg", query_heads, newest_key, preferred_element_type=jnp.float32)
        * inverse_root
    )
    overall = jnp.maximum(jnp.max(scores, axis=-1), fresh_score)
    weights_exp = jnp.exp(scores - overall[..., None])
    fresh_weight = jnp.exp(fresh_score - overall)
    denominator = jnp.sum(weights_exp, axis=-1) + fresh_weight
    mixed = jnp.einsum(
        "rkgc,rckh->rkgh", weights_exp, cached_value_rows, preferred_element_type=jnp.float32
    )
    mixed = mixed + fresh_weight[..., None] * newest_value.astype(jnp.float32)[:, :, None, :]
    mixed = (
        (mixed / denominator[..., None])
        .astype(jnp.bfloat16)
        .reshape(row_count, local_heads, group_width)
    )
    attention = lax.all_to_all(mixed, "tensor", split_axis=2, concat_axis=0, tiled=True)
    slot_ids = adapters_by_group[0]
    adapter_total = adapter_store_row.shape[0]
    matches = slot_ids[:, None] == jnp.arange(adapter_total, dtype=jnp.int32)[None, :]
    slot_home = jnp.sum(jnp.where(matches, adapter_store_row[None, :], 0), axis=1)
    store_count = adapter_down_weight.shape[0]
    slot_match = (adapter_per_row[:, None] == slot_ids[None, :]).astype(jnp.float32)
    position = slot_home - owner_index * store_count
    is_present = (position >= 0) & (position < store_count)
    clamped_index = jnp.clip(position, 0, store_count - 1)
    down_projected = jnp.where(
        is_present[:, None, None, None], adapter_down_weight[clamped_index], 0
    )
    up_projected = jnp.where(is_present[:, None, None], adapter_up_weight[clamped_index], 0)
    down_total, up_total = (
        lax.psum_scatter(down_projected, "owner", scatter_dimension=1, tiled=True).astype(
            jnp.float32
        ),
        lax.psum_scatter(up_projected, "owner", scatter_dimension=2, tiled=True).astype(
            jnp.float32
        ),
    )
    slot_down = down_total.astype(jnp.bfloat16)
    slot_up = up_total.astype(jnp.bfloat16)
    rank_slots = jnp.einsum(
        "rkf,skfn->rsn", attention, slot_down, preferred_element_type=jnp.float32
    )
    rank_part = jnp.sum(slot_match[:, :, None] * rank_slots, axis=1)
    rank_code = lax.psum(rank_part, ("tensor", "owner")).astype(jnp.bfloat16)
    update_slots = jnp.einsum("rn,snc->rsc", rank_code, slot_up, preferred_element_type=jnp.float32)
    adapter_delta = jnp.sum(slot_match[:, :, None] * update_slots, axis=1)
    partial_sum = jnp.einsum(
        "rkf,kfd->rd", attention, output_weight, preferred_element_type=jnp.float32
    )
    base_output = lax.psum_scatter(
        partial_sum, ("tensor", "owner"), scatter_dimension=1, tiled=True
    )
    return (base_output + ADAPTER_SCALE * adapter_delta).astype(jnp.bfloat16)


def solution(mesh):
    return jax.shard_map(
        shards,
        mesh=mesh,
        in_specs=(
            P(("dp", "tensor"), "owner"),
            P(("dp", "tensor"), None, "owner", None),
            P(("dp", "tensor"), None, "owner", None),
            P(("dp", "tensor"), "owner", None),
            P(("dp", "tensor"), "owner", None),
            P("owner", "tensor", None),
            P("owner", None, "tensor", None),
            P("owner", None, "tensor"),
            P(),
            P("dp", None),
            P("dp"),
        ),
        out_specs=P("dp", ("tensor", "owner")),
        check_vma=False,
    )
```

profile of v0, /device:TPU:8, one launch (start us, length us, event | category | flops | bytes accessed | tf_op | source)
XLA Modules:
  0.0 342.8 jit_solution(8786427746575031881)
XLA Ops:
  6.5 1.0 select_reduce_fusion
  7.6 4.3 %gather_fusion = bf16[16,8,64,64]{3,2,1,0:T(8,128)(2,1)} fusion(bf16[32,8,64,64]{3,2,1,0:T(8,128)(2,1)} %param.17, s32[1024]{0:T(1024)S(1)} %pad_clamp_fusion), kind=kCustom, calls=%fused_computation | custom fusion | bytes 2097216 | tf_op jit(solution)/shard_map/gather | solution.py:63
  11.9 3.1 broadcast_select_fusion
  15.1 3.2 gather_fusion.1
  18.3 1.4 broadcast_select_fusion.1
  19.7 2.9 copy.60
  22.6 4.2 %reshape.104 = bf16[512,1024]{1,0:T(8,128)(2,1)} reshape(bf16[512,16,64]{2,1,0:T(8,128)(2,1)} %bitcast.44) | data formatting | bytes 2097152
  27.0 2.4 fusion.34
  29.5 0.2 fusion.21
  29.8 0.5 fusion.16
  30.2 0.3 copy.54
  30.5 0.5 reshape.107
  31.1 16.3 %all_to_all.18 = bf16[16,2,512]{2,1,0:T(2,128)(2,1)S(1)} all-to-all(bf16[16,2,512]{2,1,0:T(2,128)(2,1)S(1)} %reshape.107), channel_id=1, replica_groups=mesh['dp'=4,'tensor'=16,'owner'=4] {'tensor'}, dimensions={0} | all-to-all | bytes 65536 | tf_op jit(solution)/shard_map/all_to_all | solution.py:52
  47.3 0.6 reshape.108
  48.0 0.4 copy.56
  48.4 2.7 convolution_bitcast_fusion
  51.1 0.6 copy-done.7
  51.7 0.6 dynamic-slice
  53.1 28.9 %all-reduce.3.cloned.1.call-done = bf16[16,8,64,64]{3,2,1,0:T(8,128)(2,1)} async-done(((bf16[16,8,64,64]{3,2,1,0:T(8,128)(2,1)}), bf16[16,8,64,64]{3,2,1,0:T(8,128)(2,1)}) %all-reduce.3.cloned.1.call-update) | async-done | bytes 1048592
  81.9 1.4 fusion.6
  83.3 249.7 %psum.7 = bf16[128,64]{0,1:T(8,128)(2,1)S(1)} all-reduce(f32[128,64]{0,1:T(8,128)S(1)} %fusion.6), channel_id=1, replica_groups=mesh['dp'=4,'tensor'=16,'owner'=4] {'tensor','owner'}, use_global_device_ids=true, to_apply=%region_6.7 | all-reduce | flops 8192 | bytes 49152 | tf_op jit(solution)/shard_map/psum | solution.py:80
  333.0 1.3 reshape.105
  334.4 0.4 fusion.4
  334.8 1.5 add_convert_fusion
  (31 shorter events, 0.5 us)
Async XLA Ops:
  6.5 41.8 %copy-start = (bf16[2,64,8192]{2,1,0:T(8,128)(2,1)S(1)}, bf16[2,64,8192]{2,1,0:T(8,128)(2,1)}, u32[]{:S(2)}) copy-start(bf16[2,64,8192]{2,1,0:T(8,128)(2,1)} %param.16) | copy-start | bytes 6291460
  6.5 75.4 %all-reduce.3.cloned.1.call-start = ((), (), s32[]{:S(2)}) async-start(), calls=%async_computation.5 | async-start | bytes 4194304
  15.1 317.9 %reduce-scatter.8.cloned.1.call-start = ((), (), s32[]{:S(2)}) async-start(), calls=%async_computation.4 | async-start | bytes 1310720
  22.6 4.2 %copy-start.2 = (bf16[8,2,128]{2,1,0:T(2,128)(2,1)S(1)}, bf16[8,2,128]{2,1,0:T(2,128)(2,1)}, u32[]{:S(2)}) copy-start(bf16[8,2,128]{2,1,0:T(2,128)(2,1)} %param.15) | copy-start | bytes 12292
  22.6 4.3 %copy-start.1 = (bf16[8,2048]{1,0:T(8,128)(2,1)S(1)}, bf16[8,2048]{1,0:T(8,128)(2,1)}, u32[]{:S(2)}) copy-start(bf16[8,2048]{1,0:T(8,128)(2,1)} %param.11) | copy-start | bytes 98308
  22.6 4.3 %copy-start.6 = (bf16[8,2,128]{2,1,0:T(2,128)(2,1)S(1)}, bf16[8,2,128]{2,1,0:T(2,128)(2,1)}, u32[]{:S(2)}) copy-start(bf16[8,2,128]{2,1,0:T(2,128)(2,1)} %param.14) | copy-start | bytes 12292
  26.8 308.0 %reduce-scatter.6.cloned.1.call-start = ((), (), s32[]{:S(2)}) async-start(), calls=%async_computation.3 | async-start | bytes 4259840 | tf_op jit(solution)/shard_map/reduce_scatter | solution.py:86
  26.9 2.9 copy-start.5
  51.0 0.7 copy-start.7
  51.0 1.9 copy-start.3
  51.0 1.9 copy-start.4
Sparse Core Ops, SparseCore 0:
  15.2 66.6 all-reduce.2
  84.6 25.9 reduce-scatter.7
  114.8 143.6 reduce-scatter.5
where the time goes:
time: 343 us
  blocking collectives  266 us (78%)
  waiting for transfers between devices  28.9 us (8%)
  local copies, waits for them, and re-layouts  19 us (6%)
  between operations  13.9 us (4%)
  matrix products  7.54 us (2%)
  other arithmetic  7.3 us (2%)
    psum x1, blocking collectives, shards(): rank_code = lax.psum(rank_part, ('tensor', 'owner')).astype(jnp.bfloat16)  250 us
    unnamed x5, waiting for transfers between devices  28.9 us
    all_to_all x1, blocking collectives, shards(): lax.all_to_all(mixed, 'tensor', split_axis=2, concat_axis=0, tiled=True)  16.3 us
    unnamed x22, local copies, waits for them, and re-layouts  10.8 us
  transfers between devices with their start and end apart: 3, of which 1 were waited for; matrix products, arithmetic and copies ran while one was open for 7% of the time, Pallas kernels for 0%

commit v1 on v0

--- a/solution.py
+++ b/solution.py
@@ -77,7 +77,10 @@
         "rkf,skfn->rsn", attention, slot_down, preferred_element_type=jnp.float32
     )
     rank_part = jnp.sum(slot_match[:, :, None] * rank_slots, axis=1)
-    rank_code = lax.psum(rank_part, ("tensor", "owner")).astype(jnp.bfloat16)
+    drive_sector_in = lambda obj, along_axis, link_axis: lax.psum(
+        lax.psum(obj, along_axis), link_axis
+    )
+    rank_code = drive_sector_in(rank_part, "tensor", "owner").astype(jnp.bfloat16)
     update_slots = jnp.einsum("rn,snc->rsc", rank_code, slot_up, preferred_element_type=jnp.float32)
     adapter_delta = jnp.sum(slot_match[:, :, None] * update_slots, axis=1)
     partial_sum = jnp.einsum(

time: 343 us -> 267 us (0.78)
  blocking collectives: 266 us -> 80.6 us
  waiting for transfers between devices: 28.9 us -> 138 us
    psum x1 -> x2, blocking collectives: 250 us -> 64.3 us  [the longest x1 48.7 us: shards(): lax.psum(obj, along_axis)]
    reduce_scatter x1, waiting for transfers between devices: 0.02 us -> 109 us  [shards(): lax.psum_scatter(partial_sum, ('tensor', 'owner'), scatter_dimension=1, t...]
  transfers between devices with their start and end apart: 3 -> 3, of which waited for: 1 -> 2; matrix products, arithmetic and copies ran while one was open for 7% -> 9% of each run, Pallas kernels for 0% -> 0%
where the time goes in v1:
time: 267 us; the launch traced here: 266 us
  waiting for transfers between devices  138 us (52%)
  blocking collectives  80.6 us (30%)
  local copies, waits for them, and re-layouts  19 us (7%)
  between operations  13.9 us (5%)
  matrix products  7.53 us (3%)
  other arithmetic  7.3 us (3%)
    reduce_scatter x1, waiting for transfers between devices, shards(): lax.psum_scatter(partial_sum, ('tensor', 'owner'), scatter_dimension=1, t...  109 us
    psum x1, blocking collectives, shards(): lax.psum(obj, along_axis)  48.7 us
    unnamed x5, waiting for transfers between devices  28.9 us
    all_to_all x1, blocking collectives, shards(): lax.all_to_all(mixed, 'tensor', split_axis=2, concat_axis=0, tiled=True)  16.3 us
    psum x1, blocking collectives, shards(): lax.psum(lax.psum(obj, along_axis), link_axis)  15.6 us
    unnamed x22, local copies, waits for them, and re-layouts  10.8 us
  transfers between devices with their start and end apart: 3, of which 2 were waited for; matrix products, arithmetic and copies ran while one was open for 9% of the time, Pallas kernels for 0%

profile of v1, /device:TPU:8, one launch (start us, length us, event | category | flops | bytes accessed | tf_op | source)
XLA Modules:
  0.0 266.4 jit_solution(18204282053482980457)
XLA Ops:
  6.5 1.0 select_reduce_fusion
  7.6 4.3 %gather_fusion = bf16[16,8,64,64]{3,2,1,0:T(8,128)(2,1)} fusion(bf16[32,8,64,64]{3,2,1,0:T(8,128)(2,1)} %param.17, s32[1024]{0:T(1024)S(1)} %pad_clamp_fusion), kind=kCustom, calls=%fused_computation | custom fusion | bytes 2097216 | tf_op jit(solution)/shard_map/gather | solution.py:63
  11.9 3.1 %broadcast_select_fusion = bf16[16,8,64,64]{3,2,1,0:T(8,128)(2,1)} fusion(bf16[16,8,64,64]{3,2,1,0:T(8,128)(2,1)} %gather_fusion, pred[16]{0:T(512)(128)(4,1)S(1)} %compare_and_fusion), kind=kLoop, calls=%fused_computation.7 | loop fusion | flops 524288 | bytes 2097168 | tf_op jit(solution)/shard_map/jit(_where)/select_n | solution.py:62
  15.1 3.2 %gather_fusion.1 = bf16[16,64,512]{2,1,0:T(8,128)(2,1)} fusion(bf16[32,64,512]{2,1,0:T(8,128)(2,1)} %param.18, s32[1024]{0:T(1024)S(1)} %pad_clamp_fusion), kind=kCustom, calls=%fused_computation.1 | custom fusion | bytes 2097216 | tf_op jit(solution)/shard_map/gather | solution.py:65
  18.3 1.4 broadcast_select_fusion.1
  19.7 2.9 %copy.60 = bf16[16,64,512]{1,0,2:T(8,128)(2,1)} copy(bf16[16,64,512]{2,1,0:T(8,128)(2,1)S(1)} %broadcast_select_fusion.1) | data formatting | bytes 2097152
  22.6 4.2 %reshape.104 = bf16[512,1024]{1,0:T(8,128)(2,1)} reshape(bf16[512,16,64]{2,1,0:T(8,128)(2,1)} %bitcast.44) | data formatting | bytes 2097152
  27.0 2.4 fusion.34
  29.8 0.5 fusion.16
  30.5 0.5 reshape.107
  31.1 16.3 %all_to_all.18 = bf16[16,2,512]{2,1,0:T(2,128)(2,1)S(1)} all-to-all(bf16[16,2,512]{2,1,0:T(2,128)(2,1)S(1)} %reshape.107), channel_id=1, replica_groups=mesh['dp'=4,'tensor'=16,'owner'=4] {'tensor'}, dimensions={0} | all-to-all | bytes 65536 | tf_op jit(solution)/shard_map/all_to_all | solution.py:52
  47.3 0.6 reshape.108
  48.0 0.4 copy.56
  48.4 2.7 %convolution_bitcast_fusion = f32[128,8192]{1,0:T(8,128)} fusion(bf16[2,64,8192]{2,1,0:T(8,128)(2,1)S(1)} %copy-done, bf16[8,2,16,64]{3,0,2,1:T(8,128)(2,1)S(1)} %copy.56), kind=kOutput, calls=%fused_computation.2 | convolution fusion | flops 268435456 | bytes 6324224 | tf_op jit(solution)/shard_map/rkf,kfd->rd/dot_general | solution.py:86
  51.1 0.6 copy-done.7
  51.7 0.6 dynamic-slice
  53.1 28.9 %all-reduce.3.cloned.1.call-done = bf16[16,8,64,64]{3,2,1,0:T(8,128)(2,1)} async-done(((bf16[16,8,64,64]{3,2,1,0:T(8,128)(2,1)}), bf16[16,8,64,64]{3,2,1,0:T(8,128)(2,1)}) %all-reduce.3.cloned.1.call-update) | async-done | bytes 1048592
  81.9 1.4 fusion.6
  83.3 48.7 %psum.14 = f32[128,64]{0,1:T(8,128)S(1)} all-reduce(f32[128,64]{0,1:T(8,128)S(1)} %fusion.6), channel_id=1, replica_groups=mesh['dp'=4,'tensor'=16,'owner'=4] {'tensor'}, use_global_device_ids=true, to_apply=%region_6.7 | all-reduce | flops 8192 | bytes 65536 | tf_op jit(solution)/shard_map/psum | solution.py:81
  132.0 15.6 %psum.15 = bf16[128,64]{0,1:T(8,128)(2,1)S(1)} all-reduce(f32[128,64]{0,1:T(8,128)S(1)} %psum.14), channel_id=1, replica_groups=mesh['dp'=4,'tensor'=16,'owner'=4] {'owner'}, use_global_device_ids=true, to_apply=%region_7.8 | all-reduce | flops 8192 | bytes 49152 | tf_op jit(solution)/shard_map/psum | solution.py:80
  147.6 1.3 reshape.105
  149.0 0.4 fusion.4
  149.4 109.0 %reduce-scatter.6.cloned.1.call-done = f32[128,128]{1,0:T(8,128)} async-done(((f32[128,8192]{1,0:T(8,128)}), f32[128,128]{1,0:T(8,128)}) %reduce-scatter.6.cloned.1.call-update) | async-done | bytes 65552 | tf_op jit(solution)/shard_map/reduce_scatter | solution.py:89
  258.4 1.5 add_convert_fusion
  (32 shorter events, 1.0 us)
Async XLA Ops:
  6.5 41.8 %copy-start = (bf16[2,64,8192]{2,1,0:T(8,128)(2,1)S(1)}, bf16[2,64,8192]{2,1,0:T(8,128)(2,1)}, u32[]{:S(2)}) copy-start(bf16[2,64,8192]{2,1,0:T(8,128)(2,1)} %param.16) | copy-start | bytes 6291460
  6.5 75.4 %all-reduce.3.cloned.1.call-start = ((), (), s32[]{:S(2)}) async-start(), calls=%async_computation.5 | async-start | bytes 4194304
  15.1 132.5 %reduce-scatter.8.cloned.1.call-start = ((), (), s32[]{:S(2)}) async-start(), calls=%async_computation.4 | async-start | bytes 1310720
  22.6 4.2 %copy-start.2 = (bf16[8,2,128]{2,1,0:T(2,128)(2,1)S(1)}, bf16[8,2,128]{2,1,0:T(2,128)(2,1)}, u32[]{:S(2)}) copy-start(bf16[8,2,128]{2,1,0:T(2,128)(2,1)} %param.15) | copy-start | bytes 12292
  22.6 4.3 %copy-start.1 = (bf16[8,2048]{1,0:T(8,128)(2,1)S(1)}, bf16[8,2048]{1,0:T(8,128)(2,1)}, u32[]{:S(2)}) copy-start(bf16[8,2048]{1,0:T(8,128)(2,1)} %param.11) | copy-start | bytes 98308
  22.6 4.3 %copy-start.6 = (bf16[8,2,128]{2,1,0:T(2,128)(2,1)S(1)}, bf16[8,2,128]{2,1,0:T(2,128)(2,1)}, u32[]{:S(2)}) copy-start(bf16[8,2,128]{2,1,0:T(2,128)(2,1)} %param.14) | copy-start | bytes 12292
  26.8 231.6 %reduce-scatter.6.cloned.1.call-start = ((), (), s32[]{:S(2)}) async-start(), calls=%async_computation.3 | async-start | bytes 4259840 | tf_op jit(solution)/shard_map/reduce_scatter | solution.py:89
  26.9 2.9 %copy-start.5 = (bf16[8,512,2,128]{3,2,1,0:T(2,128)(2,1)S(1)}, bf16[8,512,2,128]{3,2,1,0:T(2,128)(2,1)}, u32[]{:S(2)}) copy-start(bf16[8,512,2,128]{3,2,1,0:T(2,128)(2,1)} %param.13) | copy-start | bytes 6291460
  51.0 0.7 copy-start.7
  51.0 1.9 copy-start.3
  51.0 1.9 copy-start.4
Sparse Core Ops, SparseCore 0:
  15.2 66.6 all-reduce.2
  84.6 25.8 reduce-scatter.7
  114.7 143.6 reduce-scatter.5
